TPU v7x, 256 devices: a whole 4x4x8 slice. The times are simulated.
256 devices in a mesh: layer: 4 (over y_lo, core), phi: 64 (over y_hi, z, x).
Axes of the slice: x: 4, y: 4 (y_hi: 2, y_lo: 2; y = y_hi * 2 + y_lo), z: 8, core: 2. Of those that a mesh axis runs over, the one named last changes fastest.
Arguments:
- hit_features: bfloat16 [4, 64, 1024, 128], P('layer', 'phi'), may hold values from -6 to 6
- edge_features: bfloat16 [4, 64, 4, 1024, 128], P('layer', 'phi'), may hold values from -6 to 6
- sender_slot: int32 [4, 64, 4, 1024], P('layer', 'phi'), may hold values from 0 to 1023
- receiver_slot: int32 [4, 64, 4, 1024], P('layer', 'phi'), may hold values from 0 to 1023
- edge_count: int32 [4, 64, 4], P('layer', 'phi'), may hold values from 0 to 1024, as said below
- grad_hits: bfloat16 [4, 64, 1024, 128], P('layer', 'phi'), may hold values from -6 to 6
- grad_edges: bfloat16 [4, 64, 4, 1024, 128], P('layer', 'phi'), may hold values from -6 to 6
- w_edge_in: bfloat16 [384, 128], replicated, may hold values from -0.3125 to 0.3125
- w_edge_out: bfloat16 [128, 128], replicated, may hold values from -0.5 to 0.5
- w_node_in: bfloat16 [256, 128], replicated, may hold values from -0.375 to 0.375
- w_node_out: bfloat16 [128, 128], replicated, may hold values from -0.5 to 0.5
Outputs:
- hit_grads: float32 [4, 64, 1024, 128], P('layer', 'phi')
- edge_grads: bfloat16 [4, 64, 4, 1024, 128], P('layer', 'phi')
- edge_in_grad: float32 [384, 128], replicated
- edge_out_grad: float32 [128, 128], replicated
- node_in_grad: float32 [256, 128], replicated
- node_out_grad: float32 [128, 128], replicated
Inputs may be any that keep to these rules, and one draw needn't show every extreme that they name: `edge_count`: live slots come first in each block. Kind 0 edges have their sender in the same shard, kind 1 in the previous layer group, kind 2 in the previous phi sector, kind 3 in the next one (phi closes into a loop). Kind 1 has no live slots in layer group 0. Some block is full in every draw. `sender_slot`: rows of dead slots are arbitrary. `receiver_slot`: rows of dead slots are arbitrary.
All inputs are finite; a program needn't handle non-finite values.
Results may differ from a plain program's by a relative error of at most 0.009.
Values may be sent and summed in bfloat16 or wider, within the bound.
A program may use at most 64 MiB of HBM per device.

v0:
```python
import jax
import jax.numpy as jnp
from jax import lax
from jax.sharding import PartitionSpec as P

norm_eps = 1e-05


def passed_along(value, axis, steps):
    count = lax.axis_size(axis)
    initial, last = (max(0, -steps), min(count, count - steps))
    return lax.ppermute(value, axis, [(source, source + steps) for source in range(initial, last)])


def passed_along_2(block, axis, distance):
    devices = range(lax.axis_size(axis))
    route = [((i - distance) % len(devices), i) for i in devices]
    return lax.ppermute(block, axis, route)


def norm_act(pre_act):
    average = jnp.mean(pre_act, axis=-1, keepdims=True)
    centred = pre_act - average
    spread = jnp.mean(centred * centred, axis=-1, keepdims=True)
    scaled = centred * lax.rsqrt(spread + norm_eps)
    return scaled * jax.nn.sigmoid(scaled)


def norm_act_back(pre_act, upstream):
    _, pullback = jax.vjp(norm_act, pre_act)
    return pullback(upstream)[0]


def one_hot_rows(indices, node_total):
    return (indices[:, None] == lax.iota(jnp.int32, node_total)[None, :]).astype(jnp.bfloat16)


def pick_rows(selector, table):
    return jnp.dot(selector, table, preferred_element_type=jnp.float32)


def split_parts(values):
    upper = values.astype(jnp.bfloat16)
    lower = (values - upper.astype(jnp.float32)).astype(jnp.bfloat16)
    return (upper, lower)


def add_rows(selector, values):
    upper, lower = split_parts(values)
    dims = (((0,), (0,)), ((), ()))
    first = lax.dot_general(selector, upper, dims, preferred_element_type=jnp.float32)
    second = lax.dot_general(selector, lower, dims, preferred_element_type=jnp.float32)
    return first + second


def body(
    hit_features,
    edge_features,
    sender_slot,
    receiver_slot,
    edge_count,
    grad_hits,
    grad_edges,
    w_edge_in,
    w_edge_out,
    w_node_in,
    w_node_out,
):
    local_rows = hit_features[0, 0]
    node_total = local_rows.shape[0]
    features = local_rows.shape[1]
    send_all = sender_slot[0, 0]
    recv_all = receiver_slot[0, 0]
    counts = edge_count[0, 0]
    edge_all = edge_features[0, 0]
    grad_edge_all = grad_edges[0, 0]
    grad_local = grad_hits[0, 0]
    kind_total = send_all.shape[0]
    capacity = send_all.shape[1]
    tile_rows = 256
    tile_total = capacity // tile_rows
    lower_rows = passed_along(local_rows, "layer", 1)
    prev_rows = passed_along_2(local_rows, "phi", 1)
    next_rows = passed_along_2(local_rows, "phi", -1)
    sources = (local_rows, lower_rows, prev_rows, next_rows)
    positions = lax.iota(jnp.int32, capacity)
    live_all = (positions[None, :] < counts[:, None]).astype(jnp.float32)

    def tile_indices(k, offset):
        send_idx = lax.dynamic_slice_in_dim(send_all[k], offset, tile_rows, 0)
        recv_idx = lax.dynamic_slice_in_dim(recv_all[k], offset, tile_rows, 0)
        live_mask = lax.dynamic_slice_in_dim(live_all[k], offset, tile_rows, 0)
        return (send_idx, recv_idx, live_mask)

    def forward_tile(k, offset, send_hot, recv_hot):
        edge_rows = lax.dynamic_slice_in_dim(edge_all[k], offset, tile_rows, 0)
        sender_rows = pick_rows(send_hot, sources[k]).astype(jnp.bfloat16)
        receiver_rows = pick_rows(recv_hot, local_rows).astype(jnp.bfloat16)
        inputs = jnp.concatenate([sender_rows, receiver_rows, edge_rows], axis=-1)
        pre_act = jnp.dot(inputs, w_edge_in, preferred_element_type=jnp.float32)
        hidden = norm_act(pre_act).astype(jnp.bfloat16)
        return (inputs, pre_act, hidden)

    def run_tiles(tile_step, totals):

        def looped(number, inner):
            return tile_step(number * tile_rows, inner)

        return lax.fori_loop(0, tile_total, looped, totals)

    incoming = jnp.zeros((node_total, features), jnp.float32)
    stored = []
    for k in range(kind_total):

        def message_step(offset, totals):
            total, kept = totals
            send_idx, recv_idx, live_mask = tile_indices(k, offset)
            send_hot = one_hot_rows(send_idx, node_total)
            recv_hot = one_hot_rows(recv_idx, node_total)
            inputs, pre_act, hidden = forward_tile(k, offset, send_hot, recv_hot)
            message = (
                jnp.dot(hidden, w_edge_out, preferred_element_type=jnp.float32) * live_mask[:, None]
            )
            total = total + add_rows(recv_hot, message)
            kept = (
                lax.dynamic_update_slice_in_dim(kept[0], inputs, offset, 0),
                lax.dynamic_update_slice_in_dim(kept[1], pre_act, offset, 0),
                lax.dynamic_update_slice_in_dim(kept[2], hidden, offset, 0),
            )
            return (total, kept)

        kept_start = (
            jnp.zeros((capacity, 3 * features), jnp.bfloat16),
            jnp.zeros((capacity, features), jnp.float32),
            jnp.zeros((capacity, features), jnp.bfloat16),
        )
        incoming, kept_done = run_tiles(message_step, (incoming, kept_start))
        stored.append(kept_done)
    incoming = incoming.astype(jnp.bfloat16)
    node_in = jnp.concatenate([local_rows, incoming], axis=-1)
    node_pre = jnp.dot(node_in, w_node_in, preferred_element_type=jnp.float32)
    node_hidden = norm_act(node_pre).astype(jnp.bfloat16)
    node_hidden_grad = jnp.dot(grad_local, w_node_out.T, preferred_element_type=jnp.float32)
    node_out_part = jnp.dot(node_hidden.T, grad_local, preferred_element_type=jnp.float32)
    node_pre_grad = norm_act_back(node_pre, node_hidden_grad).astype(jnp.bfloat16)
    node_input_grad = jnp.dot(node_pre_grad, w_node_in.T, preferred_element_type=jnp.float32)
    node_in_part = jnp.dot(node_in.T, node_pre_grad, preferred_element_type=jnp.float32)
    incoming_upper, incoming_lower = split_parts(node_input_grad[:, features:])
    recv_total = jnp.zeros((node_total, features), jnp.float32)
    in_total = jnp.zeros((3 * features, features), jnp.float32)
    out_total = jnp.zeros((features, features), jnp.float32)
    send_parts = []
    edge_parts = []
    for k in range(kind_total):

        def back_step(offset, totals):
            recv_sum, send_sum, in_sum, out_sum, edge_done = totals
            send_idx, recv_idx, live_mask = tile_indices(k, offset)
            send_hot = one_hot_rows(send_idx, node_total)
            recv_hot = one_hot_rows(recv_idx, node_total)
            inputs = lax.dynamic_slice_in_dim(stored[k][0], offset, tile_rows, 0)
            pre_act = lax.dynamic_slice_in_dim(stored[k][1], offset, tile_rows, 0)
            hidden = lax.dynamic_slice_in_dim(stored[k][2], offset, tile_rows, 0)
            grad_rows = lax.dynamic_slice_in_dim(grad_edge_all[k], offset, tile_rows, 0)
            picked = pick_rows(recv_hot, incoming_upper) + pick_rows(recv_hot, incoming_lower)
            message_grad = (live_mask[:, None] * (grad_rows.astype(jnp.float32) + picked)).astype(
                jnp.bfloat16
            )
            hidden_grad = jnp.dot(message_grad, w_edge_out.T, preferred_element_type=jnp.float32)
            pre_grad = norm_act_back(pre_act, hidden_grad).astype(jnp.bfloat16)
            input_grad = jnp.dot(pre_grad, w_edge_in.T, preferred_element_type=jnp.float32)
            edge_new = (grad_rows.astype(jnp.float32) + input_grad[:, 2 * features :]).astype(
                jnp.bfloat16
            )
            edge_done = lax.dynamic_update_slice_in_dim(edge_done, edge_new, offset, 0)
            recv_sum = recv_sum + add_rows(recv_hot, input_grad[:, features : 2 * features])
            send_sum = send_sum + add_rows(send_hot, input_grad[:, :features])
            in_sum = in_sum + jnp.dot(inputs.T, pre_grad, preferred_element_type=jnp.float32)
            out_sum = out_sum + jnp.dot(hidden.T, message_grad, preferred_element_type=jnp.float32)
            return (recv_sum, send_sum, in_sum, out_sum, edge_done)

        start_totals = (
            recv_total,
            jnp.zeros((node_total, features), jnp.float32),
            in_total,
            out_total,
            grad_edge_all[k],
        )
        recv_total, send_sum, in_total, out_total, edge_done = run_tiles(back_step, start_totals)
        send_parts.append(send_sum)
        edge_parts.append(edge_done)
    from_upper = passed_along(send_parts[1].astype(jnp.bfloat16), "layer", -1).astype(jnp.float32)
    from_next = passed_along_2(send_parts[2].astype(jnp.bfloat16), "phi", -1).astype(jnp.float32)
    from_prev = passed_along_2(send_parts[3].astype(jnp.bfloat16), "phi", 1).astype(jnp.float32)
    returned = from_next + from_prev
    hit_total = (
        grad_local.astype(jnp.float32)
        + node_input_grad[:, :features]
        + recv_total
        + send_parts[0]
        + from_upper
        + returned
    )
    summed = lax.psum((in_total, out_total, node_in_part, node_out_part), ("layer", "phi"))
    shard_count = lax.axis_size("layer") * lax.axis_size("phi")
    edge_stack = jnp.stack(edge_parts)
    return (
        hit_total[None, None],
        edge_stack[None, None],
        summed[0] / shard_count,
        summed[1] / shard_count,
        summed[2] / shard_count,
        summed[3] / shard_count,
    )


def solution(mesh):
    placed = (
        P("layer", "phi", None, None),
        P("layer", "phi", None, None, None),
        P("layer", "phi", None, None),
        P("layer", "phi", None, None),
        P("layer", "phi", None),
        P("layer", "phi", None, None),
        P("layer", "phi", None, None, None),
        P(),
        P(),
        P(),
        P(),
    )
    return jax.shard_map(
        body,
        mesh=mesh,
        in_specs=placed,
        out_specs=(
            P("layer", "phi", None, None),
            P("layer", "phi", None, None, None),
            P(),
            P(),
            P(),
            P(),
        ),
        check_vma=False,
    )
```

profile of v0, /device:TPU:2, one launch (start us, length us, event | category | flops | bytes accessed | tf_op | source)
XLA Modules:
  0.0 593.0 jit_solution(756839716940063795)
XLA Ops:
  7.2 2.4 collective-permute-start
  9.7 1.5 collective-permute-start.1
  12.4 1.5 copy.17
  16.6 33.2 %while.168 = (s32[]{:T(128)}, f32[1024,128]{1,0:T(8,128)S(1)}, bf16[1024,384]{0,1:T(8,128)(2,1)}, f32[1024,128]{0,1:T(8,128)}, bf16[1024,128]{0,1:T(8,128)(2,1)S...) while((s32[]{:T(128)}, f32[1024,128]{1,0:T(8,128)S(1)}, ...), condition=%wide.region_3.0_spmd.clone, body=%wide.region_0.0_spmd.clone.sunk | while | flops 305463552 | bytes 8575457 | solution.py:109
  16.7 1.4 convolution_convert_fusion.22
  18.2 1.4 convolution_convert_fusion.23
  25.0 1.4 convolution_convert_fusion.22
  26.4 1.4 convolution_convert_fusion.23
  33.3 1.4 convolution_convert_fusion.22
  34.7 1.4 convolution_convert_fusion.23
  41.6 1.4 convolution_convert_fusion.22
  43.0 1.4 convolution_convert_fusion.23
  54.2 26.9 %while.165 = (s32[]{:T(128)}, f32[1024,128]{1,0:T(8,128)S(1)}, bf16[1024,384]{0,1:T(8,128)(2,1)}, f32[1024,128]{0,1:T(8,128)}, bf16[1024,128]{0,1:T(8,128)(2,1)}...) while((s32[]{:T(128)}, f32[1024,128]{1,0:T(8,128)S(1)}, ...), condition=%wide.region_7.0_spmd, body=%wide.region_4.0_spmd.sunk | while | flops 305332480 | bytes 5421311 | solution.py:109
  54.2 1.4 convolution_convert_fusion.16
  55.6 1.4 convolution_convert_fusion.17
  60.9 1.4 convolution_convert_fusion.16
  62.3 1.4 convolution_convert_fusion.17
  67.6 1.4 convolution_convert_fusion.16
  69.0 1.4 convolution_convert_fusion.17
  74.4 1.4 convolution_convert_fusion.16
  75.8 1.4 convolution_convert_fusion.17
  83.7 27.0 %while.166 = (s32[]{:T(128)}, f32[1024,128]{1,0:T(8,128)S(1)}, bf16[1024,384]{0,1:T(8,128)(2,1)}, f32[1024,128]{0,1:T(8,128)}, bf16[1024,128]{0,1:T(8,128)(2,1)}...) while((s32[]{:T(128)}, f32[1024,128]{1,0:T(8,128)S(1)}, ...), condition=%wide.region_11.0_spmd, body=%wide.region_8.0_spmd.sunk | while | flops 305332480 | bytes 5421311 | solution.py:109
  90.5 1.4 convolution_convert_fusion.18
  91.8 1.4 convolution_convert_fusion.19
  97.2 1.4 convolution_convert_fusion.18
  98.6 1.4 convolution_convert_fusion.19
  103.9 1.4 convolution_convert_fusion.18
  105.3 1.4 convolution_convert_fusion.19
  113.3 27.0 %while.167 = (s32[]{:T(128)}, f32[1024,128]{1,0:T(8,128)S(1)}, bf16[1024,384]{0,1:T(8,128)(2,1)}, f32[1024,128]{0,1:T(8,128)}, bf16[1024,128]{0,1:T(8,128)(2,1)}...) while((s32[]{:T(128)}, f32[1024,128]{1,0:T(8,128)S(1)}, ...), condition=%wide.region_15.0_spmd, body=%wide.region_12.0_spmd.sunk | while | flops 305332480 | bytes 5421311 | solution.py:109
  114.7 1.4 convolution_convert_fusion.21
  120.1 1.4 convolution_convert_fusion.20
  121.5 1.4 convolution_convert_fusion.21
  126.8 1.4 convolution_convert_fusion.20
  128.2 1.4 convolution_convert_fusion.21
  133.6 1.4 convolution_convert_fusion.20
  134.9 1.4 convolution_convert_fusion.21
  144.1 1.9 fusion.147
  148.2 51.9 %while.169 = (s32[]{:T(128)}, f32[1024,128]{1,0:T(8,128)S(1)}, f32[1024,128]{1,0:T(8,128)}, f32[384,128]{1,0:T(8,128)S(1)}, f32[128,128]{1,0:T(8,128)S(1)}, /*in...) while((s32[]{:T(128)}, f32[1024,128]{1,0:T(8,128)S(1)}, ...), condition=%wide.region_25.26_spmd.clone, body=%wide.region_20.25_spmd.clone.sunk | while | flops 473990912 | bytes 11069784 | solution.py:109
  148.2 1.4 fusion.369
  154.9 1.4 fusion.376
  167.1 2.4 fusion.376
  180.4 2.4 fusion.376
  193.6 2.4 fusion.376
  200.1 40.0 %while.170 = (s32[]{:T(128)}, f32[1024,128]{1,0:T(8,128)S(1)}, f32[1024,128]{1,0:T(8,128)}, f32[384,128]{1,0:T(8,128)S(1)}, f32[128,128]{1,0:T(8,128)S(1)}, /*in...) while((s32[]{:T(128)}, f32[1024,128]{1,0:T(8,128)S(1)}, ...), condition=%wide.region_31.0_spmd.clone, body=%wide.region_26.31_spmd.clone.sunk | while | flops 473794304 | bytes 13166961 | solution.py:109
  203.9 1.4 fusion.394
  213.1 2.4 fusion.394
  223.4 2.4 fusion.394
  233.6 2.4 fusion.394
  240.1 39.9 %while.171 = (s32[]{:T(128)}, f32[1024,128]{1,0:T(8,128)S(1)}, f32[1024,128]{1,0:T(8,128)}, f32[384,128]{1,0:T(8,128)S(1)}, f32[128,128]{1,0:T(8,128)S(1)}, /*in...) while((s32[]{:T(128)}, f32[1024,128]{1,0:T(8,128)S(1)}, ...), condition=%wide.region_37.38_spmd.clone, body=%wide.region_32.37_spmd.clone.sunk | while | flops 473794304 | bytes 13166961 | solution.py:109
  243.9 1.4 fusion.412
  253.1 2.4 fusion.412
  263.3 2.4 fusion.412
  273.6 2.4 fusion.412
  280.1 39.9 %while.172 = (s32[]{:T(128)}, f32[1024,128]{1,0:T(8,128)S(1)}, f32[1024,128]{1,0:T(8,128)}, f32[384,128]{1,0:T(8,128)S(1)}, f32[128,128]{1,0:T(8,128)S(1)}, /*in...) while((s32[]{:T(128)}, f32[1024,128]{1,0:T(8,128)S(1)}, ...), condition=%wide.region_43.44_spmd.clone, body=%wide.region_38.43_spmd.clone.sunk | while | flops 473794304 | bytes 13166961 | solution.py:109
  293.0 2.4 fusion.430
  303.2 2.4 fusion.430
  313.5 2.4 fusion.430
  320.7 1.8 convert_element_type.565
  322.4 1.5 collective-permute-start.5
  324.7 7.7 %collective-permute-start.4 = (bf16[1024,128]{1,0:T(8,128)(2,1)}, bf16[1024,128]{1,0:T(8,128)(2,1)S(1)}, u32[]{:S(2)}, u32[]{:S(2)}) collective-permute-start(bf16[1024,128]{1,0:T(8,128)(2,1)} %convert_element_type.563), channel_id=1, source_target_pairs={{1,0},{2,1},{3,2},{4,3},{5,4},{6,5},{7,6},{8,7},{9,8},{10,9},{11,1... | collective-permute-start | bytes 786440 | tf_op jit(solution)/shard_map/ppermute | solution.py:18
  335.6 244.9 %all-reduce.3.cloned.1.call-done = (f32[384,128]{1,0:T(8,128)}, f32[128,128]{1,0:T(8,128)}, f32[256,128]{1,0:T(8,128)}, f32[128,128]{1,0:T(8,128)}) async-done(((f32[384,128]{1,0:T(8,128)}, f32[128,128]{1,0:T(8,128)}, f32[256,128]{1,0:T(8,128)}, f32[128,128]{1,0:T(8,128)}), (f32[384,128]{1,0:T(8,128)}, f32[128,128]{1,0:T(8,128)}, f32[256,128]{1,0:T(8,128)}, ...) | async-done | bytes 458768 | tf_op jit(solution)/shard_map/psum | solution.py:204
  580.4 1.6 broadcast_multiply_fusion.9
  582.0 1.5 broadcast_multiply_fusion.10
  583.5 1.7 broadcast_multiply_fusion.8
  (906 shorter events, 232.6 us)
Async XLA Ops:
  7.2 133.1 %copy-start = (bf16[256,128]{1,0:T(8,128)(2,1)S(1)}, bf16[256,128]{1,0:T(8,128)(2,1)}, u32[]{:S(2)}) copy-start(bf16[256,128]{1,0:T(8,128)(2,1)} %param.36) | copy-start | bytes 196612
  7.2 573.2 %all-reduce.3.cloned.1.call-start = ((), (), s32[]{:S(2)}) async-start(), calls=%async_computation | async-start | bytes 917504 | tf_op jit(solution)/shard_map/psum | solution.py:204
  7.2 44.3 %collective-permute-start = (bf16[1024,128]{1,0:T(8,128)(2,1)}, bf16[1024,128]{1,0:T(8,128)(2,1)}, u32[]{:S(2)}, u32[]{:S(2)}) collective-permute-start(bf16[1024,128]{1,0:T(8,128)(2,1)} %bitcast.13), channel_id=1, source_target_pairs={{0,64},{64,128},{128,192},{1,65},{65,129},{129,193},{2,66},{66,130... | collective-permute-start | bytes 786440 | tf_op jit(solution)/shard_map/ppermute | solution.py:12
  9.7 71.4 %collective-permute-start.1 = (bf16[1024,128]{1,0:T(8,128)(2,1)}, bf16[1024,128]{1,0:T(8,128)(2,1)}, u32[]{:S(2)}, u32[]{:S(2)}) collective-permute-start(bf16[1024,128]{1,0:T(8,128)(2,1)} %bitcast.13), channel_id=1, source_target_pairs={{63,0},{0,1},{1,2},{2,3},{3,4},{4,5},{5,6},{6,7},{7,8},{8,9},{9,10... | collective-permute-start | bytes 786440 | tf_op jit(solution)/shard_map/ppermute | solution.py:18
  11.2 99.5 %collective-permute-start.2 = (bf16[1024,128]{1,0:T(8,128)(2,1)}, bf16[1024,128]{1,0:T(8,128)(2,1)}, u32[]{:S(2)}, u32[]{:S(2)}) collective-permute-start(bf16[1024,128]{1,0:T(8,128)(2,1)} %bitcast.13), channel_id=1, source_target_pairs={{1,0},{2,1},{3,2},{4,3},{5,4},{6,5},{7,6},{8,7},{9,8},{10,9},{11,1... | collective-permute-start | bytes 786440 | tf_op jit(solution)/shard_map/ppermute | solution.py:18
  16.6 33.9 %copy-start.3 = (bf16[1,1,4,1024,128]{4,3,2,1,0:T(8,128)(2,1)S(1)}, bf16[1,1,4,1024,128]{4,3,2,1,0:T(8,128)(2,1)}, u32[]{:S(2)}) copy-start(bf16[1,1,4,1024,128]{4,3,2,1,0:T(8,128)(2,1)} %param.33) | copy-start | bytes 3145732
  16.7 5.4 copy-start.37
  18.1 1.5 copy-start.16
  25.0 5.4 copy-start.37
  26.4 1.5 copy-start.16
  33.3 5.4 copy-start.37
  34.7 1.5 copy-start.16
  41.6 5.4 copy-start.37
  43.0 1.5 copy-start.16
  148.2 1.5 copy-start.29
  159.3 1.1 copy-start.30
  160.4 1.5 copy-start.29
  172.6 1.1 copy-start.30
  173.7 1.5 copy-start.29
  185.8 1.1 copy-start.30
  186.9 1.5 copy-start.29
  199.1 1.1 copy-start.30
  200.1 1.5 copy-start.31
  201.6 1.0 copy-start.10
  208.3 1.0 copy-start.32
  209.4 1.5 copy-start.31
  210.8 1.0 copy-start.10
  218.6 1.0 copy-start.32
  219.6 1.5 copy-start.31
  221.1 1.0 copy-start.10
  228.8 1.0 copy-start.32
  229.9 1.5 copy-start.31
  231.3 1.0 copy-start.10
  239.1 1.0 copy-start.32
  240.1 1.5 copy-start.33
  241.6 1.0 copy-start.11
  248.3 1.0 copy-start.34
  249.3 1.5 copy-start.33
  250.8 1.0 copy-start.11
  258.5 1.0 copy-start.34
  259.6 1.5 copy-start.33
  261.0 1.0 copy-start.11
  269.8 1.5 copy-start.33
  271.3 1.0 copy-start.11
  280.1 1.5 copy-start.35
  281.5 1.0 copy-start.9
  289.3 1.5 copy-start.35
  290.7 1.0 copy-start.9
  299.5 1.5 copy-start.35
  301.0 1.0 copy-start.9
  309.7 1.5 copy-start.35
  311.2 1.0 copy-start.9
  320.0 3.9 copy-start.6
  322.4 9.9 %copy-start.7 = (f32[1024,128]{1,0:T(8,128)S(1)}, f32[1024,128]{1,0:T(8,128)}, u32[]{:S(2)}) copy-start(f32[1024,128]{1,0:T(8,128)} %get-tuple-element.1998) | copy-start | bytes 1572868
  322.4 262.7 %collective-permute-start.5 = (bf16[1024,128]{1,0:T(8,128)(2,1)}, bf16[1024,128]{1,0:T(8,128)(2,1)S(1)}, u32[]{:S(2)}, u32[]{:S(2)}) collective-permute-start(bf16[1024,128]{1,0:T(8,128)(2,1)} %convert_element_type.565), channel_id=1, source_target_pairs={{63,0},{0,1},{1,2},{2,3},{3,4},{4,5},{5,6},{6,7},{7,8},{8,9},{9,10... | collective-permute-start | bytes 786440 | tf_op jit(solution)/shard_map/ppermute | solution.py:18
  323.9 10.5 %copy-start.26 = (bf16[1024,128]{1,0:T(8,128)(2,1)S(1)}, bf16[1024,128]{1,0:T(8,128)(2,1)}, u32[]{:S(2)}) copy-start(bf16[1024,128]{1,0:T(8,128)(2,1)} %get-tuple-element.2001) | copy-start | bytes 786436
  324.7 260.5 %collective-permute-start.4 = (bf16[1024,128]{1,0:T(8,128)(2,1)}, bf16[1024,128]{1,0:T(8,128)(2,1)S(1)}, u32[]{:S(2)}, u32[]{:S(2)}) collective-permute-start(bf16[1024,128]{1,0:T(8,128)(2,1)} %convert_element_type.563), channel_id=1, source_target_pairs={{1,0},{2,1},{3,2},{4,3},{5,4},{6,5},{7,6},{8,7},{9,8},{10,9},{11,1... | collective-permute-start | bytes 786440 | tf_op jit(solution)/shard_map/ppermute | solution.py:18
  332.4 2.0 copy-start.23
  332.4 2.0 copy-start.24
  332.4 2.1 copy-start.25
  333.1 252.1 %collective-permute-start.3 = (bf16[1024,128]{1,0:T(8,128)(2,1)}, bf16[1024,128]{1,0:T(8,128)(2,1)S(1)}, u32[]{:S(2)}, u32[]{:S(2)}) collective-permute-start(bf16[1024,128]{1,0:T(8,128)(2,1)} %convert_element_type.561), channel_id=1, source_target_pairs={{64,0},{128,64},{192,128},{65,1},{129,65},{193,129},{66,2},{130,66... | collective-permute-start | bytes 786440 | tf_op jit(solution)/shard_map/ppermute | solution.py:12
  334.4 250.7 %copy-start.13 = (f32[1024,256]{1,0:T(8,128)S(1)}, f32[1024,256]{1,0:T(8,128)}, u32[]{:S(2)}) copy-start(f32[1024,256]{1,0:T(8,128)} %copy-done.12) | copy-start | bytes 3145732
  335.6 249.6 %copy-start.8 = (f32[1024,128]{1,0:T(8,128)S(1)}, f32[1024,128]{1,0:T(8,128)}, u32[]{:S(2)}) copy-start(f32[1024,128]{1,0:T(8,128)} %get-tuple-element.1997) | copy-start | bytes 1572868
  583.5 1.7 copy-start.28
  (58 other events, 47.1 us)
Sparse Core Ops, SparseCore 0:
  320.8 259.5 all-reduce.2
where the time goes:
time: 598 us; the launch traced here: 593 us
  waiting for transfers between devices  245 us (41%)
  matrix products  212 us (35%)
  other arithmetic  66.8 us (11%)
  local copies, waits for them, and re-layouts  36.3 us (6%)
  starting transfers between devices  15 us (3%)
  between operations  14.3 us (2%)
    psum x1, waiting for transfers between devices, body(): lax.psum((in_total, out_total, node_in_part, node_out_part), ('layer', 'p...  245 us
    dot_general x64, matrix products, pick_rows(): return jnp.dot(selector, table, preferred_element_type=jnp.float32)  71.2 us
    dot_general x48, matrix products, add_rows(): lax.dot_general(selector, lower, dims, preferred_element_type=jnp.float32)  55.7 us
    dot_general x48, matrix products, add_rows(): lax.dot_general(selector, upper, dims, preferred_element_type=jnp.float32)  26.7 us
    dot_general x16, matrix products, back_step(): jnp.dot(inputs.T, pre_grad, preferred_element_type=jnp.float32)  18.4 us
    while x184, local copies, waits for them, and re-layouts  17.3 us
    dot_general x16, matrix products, back_step(): jnp.dot(hidden.T, message_grad, preferred_element_type=jnp.float32)  16.4 us
  transfers between devices with their start and end apart: 7, of which 1 were waited for; matrix products, arithmetic and copies ran while one was open for 16% of the time, Pallas kernels for 0%

commit v1 on v0

--- a/solution.py
+++ b/solution.py
@@ -201,7 +201,9 @@
         + from_upper
         + returned
     )
-    summed = lax.psum((in_total, out_total, node_in_part, node_out_part), ("layer", "phi"))
+    summed = (in_total, out_total, node_in_part, node_out_part)
+    for mesh_axis in ("phi", "layer"):
+        summed = lax.psum(summed, mesh_axis)
     shard_count = lax.axis_size("layer") * lax.axis_size("phi")
     edge_stack = jnp.stack(edge_parts)
     return (

time: 598 us -> 1080 us (1.81)
  waiting for transfers between devices: 245 us -> 715 us
  local copies, waits for them, and re-layouts: 36.3 us -> 66.5 us
  matrix products: 212 us -> 190 us
    psum x1 -> x2, waiting for transfers between devices: 245 us -> 715 us  [body(): summed = lax.psum(summed, mesh_axis)]
    while x184 -> x376, local copies, waits for them, and re-layouts: 17.3 us -> 47.2 us
    dot_general x64, matrix products: 71.2 us -> 47.4 us  [pick_rows(): return jnp.dot(selector, table, preferred_element_type=jnp.float32)]
  transfers between devices with their start and end apart: 7 -> 8, of which waited for: 1 -> 2; matrix products, arithmetic and copies ran while one was open for 16% -> 9% of each run, Pallas kernels for 0% -> 0%
where the time goes in v1:
time: 1080 us; the launch traced here: 1070 us
  waiting for transfers between devices  715 us (66%)
  matrix products  190 us (18%)
  other arithmetic  69 us (6%)
  local copies, waits for them, and re-layouts  66.5 us (6%)
  starting transfers between devices  15.2 us (1%)
  between operations  14.3 us (1%)
    psum x2, waiting for transfers between devices, body(): summed = lax.psum(summed, mesh_axis)  715 us
    dot_general x48, matrix products, add_rows(): lax.dot_general(selector, lower, dims, preferred_element_type=jnp.float32)  59.6 us
    dot_general x64, matrix products, pick_rows(): return jnp.dot(selector, table, preferred_element_type=jnp.float32)  47.4 us
    while x376, local copies, waits for them, and re-layouts  47.2 us
    dot_general x48, matrix products, add_rows(): lax.dot_general(selector, upper, dims, preferred_element_type=jnp.float32)  26.7 us
  transfers between devices with their start and end apart: 8, of which 2 were waited for; matrix products, arithmetic and copies ran while one was open for 9% of the time, Pallas kernels for 0%

profile of v1, /device:TPU:2, one launch (start us, length us, event | category | flops | bytes accessed | tf_op | source)
XLA Modules:
  0.0 1074.6 jit_solution(5720589740726439456)
XLA Ops:
  7.2 2.5 collective-permute-start
  9.7 1.5 collective-permute-start.1
  12.4 1.5 copy.17
  16.7 31.7 %while.168 = (s32[]{:T(128)}, f32[1024,128]{1,0:T(8,128)S(1)}, bf16[1024,384]{0,1:T(8,128)(2,1)}, f32[1024,128]{0,1:T(8,128)}, bf16[1024,128]{0,1:T(8,128)(2,1)}...) while((s32[]{:T(128)}, f32[1024,128]{1,0:T(8,128)S(1)}, ...), condition=%wide.region_3.0_spmd.clone, body=%wide.region_0.0_spmd.clone.sunk | while | flops 305463552 | bytes 8051185 | solution.py:109
  22.0 1.7 fusion.358
  29.9 1.7 fusion.358
  37.8 1.7 fusion.358
  45.8 1.7 fusion.358
  52.1 27.0 %while.165 = (s32[]{:T(128)}, f32[1024,128]{1,0:T(8,128)S(1)}, bf16[1024,384]{0,1:T(8,128)(2,1)}, f32[1024,128]{0,1:T(8,128)}, bf16[1024,128]{0,1:T(8,128)(2,1)}...) while((s32[]{:T(128)}, f32[1024,128]{1,0:T(8,128)S(1)}, ...), condition=%wide.region_7.0_spmd, body=%wide.region_4.0_spmd.sunk | while | flops 305332480 | bytes 5421311 | solution.py:109
  52.1 1.4 convolution_convert_fusion.16
  53.5 1.4 convolution_convert_fusion.17
  58.9 1.4 convolution_convert_fusion.16
  60.2 1.4 convolution_convert_fusion.17
  65.6 1.4 convolution_convert_fusion.16
  67.0 1.4 convolution_convert_fusion.17
  72.4 1.4 convolution_convert_fusion.16
  73.7 1.4 convolution_convert_fusion.17
  81.7 27.0 %while.166 = (s32[]{:T(128)}, f32[1024,128]{1,0:T(8,128)S(1)}, bf16[1024,384]{0,1:T(8,128)(2,1)}, f32[1024,128]{0,1:T(8,128)}, bf16[1024,128]{0,1:T(8,128)(2,1)}...) while((s32[]{:T(128)}, f32[1024,128]{1,0:T(8,128)S(1)}, ...), condition=%wide.region_11.0_spmd, body=%wide.region_8.0_spmd.sunk | while | flops 305332480 | bytes 5421311 | solution.py:109
  81.7 1.4 convolution_convert_fusion.18
  83.1 1.4 convolution_convert_fusion.19
  88.5 1.4 convolution_convert_fusion.18
  89.9 1.4 convolution_convert_fusion.19
  95.2 1.4 convolution_convert_fusion.18
  96.6 1.4 convolution_convert_fusion.19
  102.0 1.4 convolution_convert_fusion.18
  103.4 1.4 convolution_convert_fusion.19
  111.3 27.0 %while.167 = (s32[]{:T(128)}, f32[1024,128]{1,0:T(8,128)S(1)}, bf16[1024,384]{0,1:T(8,128)(2,1)}, f32[1024,128]{0,1:T(8,128)}, bf16[1024,128]{0,1:T(8,128)(2,1)}...) while((s32[]{:T(128)}, f32[1024,128]{1,0:T(8,128)S(1)}, ...), condition=%wide.region_15.0_spmd, body=%wide.region_12.0_spmd.sunk | while | flops 305332480 | bytes 5421311 | solution.py:109
  111.3 1.4 convolution_convert_fusion.20
  112.7 1.4 convolution_convert_fusion.21
  118.0 1.4 convolution_convert_fusion.20
  119.4 1.4 convolution_convert_fusion.21
  124.8 1.4 convolution_convert_fusion.20
  126.2 1.4 convolution_convert_fusion.21
  131.5 1.4 convolution_convert_fusion.20
  132.9 1.4 convolution_convert_fusion.21
  144.5 55.4 %while.169 = (s32[]{:T(128)}, f32[1024,128]{1,0:T(8,128)S(1)}, f32[1024,128]{1,0:T(8,128)}, f32[384,128]{1,0:T(8,128)S(1)}, f32[128,128]{1,0:T(8,128)S(1)}, /*in...) while((s32[]{:T(128)}, f32[1024,128]{1,0:T(8,128)S(1)}, ...), condition=%wide.region_25.26_spmd.clone, body=%wide.region_20.25_spmd.clone.sunk | while | flops 473990912 | bytes 12265984 | solution.py:109
  152.0 1.4 fusion.376
  154.6 1.2 convolution_add_fusion.32
  165.1 2.4 fusion.376
  179.2 2.4 fusion.376
  193.3 2.4 fusion.376
  199.9 43.7 %while.170 = (s32[]{:T(128)}, f32[1024,128]{1,0:T(8,128)S(1)}, f32[1024,128]{1,0:T(8,128)}, f32[384,128]{1,0:T(8,128)S(1)}, f32[128,128]{1,0:T(8,128)S(1)}, /*in...) while((s32[]{:T(128)}, f32[1024,128]{1,0:T(8,128)S(1)}, ...), condition=%wide.region_31.0_spmd.clone, body=%wide.region_26.31_spmd.clone.sunk | while | flops 473794304 | bytes 14363161 | solution.py:109
  204.5 1.4 fusion.394
  214.7 2.4 fusion.394
  225.9 2.4 fusion.394
  237.1 2.4 fusion.394
  243.6 43.7 %while.171 = (s32[]{:T(128)}, f32[1024,128]{1,0:T(8,128)S(1)}, f32[1024,128]{1,0:T(8,128)}, f32[384,128]{1,0:T(8,128)S(1)}, f32[128,128]{1,0:T(8,128)S(1)}, /*in...) while((s32[]{:T(128)}, f32[1024,128]{1,0:T(8,128)S(1)}, ...), condition=%wide.region_37.38_spmd.clone, body=%wide.region_32.37_spmd.clone.sunk | while | flops 473794304 | bytes 14363161 | solution.py:109
  248.2 1.4 fusion.412
  258.4 2.4 fusion.412
  269.6 2.4 fusion.412
  280.8 2.4 fusion.412
  287.3 43.7 %while.172 = (s32[]{:T(128)}, f32[1024,128]{1,0:T(8,128)S(1)}, f32[1024,128]{1,0:T(8,128)}, f32[384,128]{1,0:T(8,128)S(1)}, f32[128,128]{1,0:T(8,128)S(1)}, /*in...) while((s32[]{:T(128)}, f32[1024,128]{1,0:T(8,128)S(1)}, ...), condition=%wide.region_43.44_spmd.clone, body=%wide.region_38.43_spmd.clone.sunk | while | flops 473794304 | bytes 14363161 | solution.py:109
  291.9 1.4 fusion.430
  302.1 2.4 fusion.430
  313.2 2.4 fusion.430
  324.4 2.4 fusion.430
  331.7 1.8 convert_element_type.565
  333.5 1.5 collective-permute-start.5
  335.7 7.7 collective-permute-start.4
  344.1 1.4 collective-permute-start.3
  345.6 673.1 %all-reduce.5.cloned.1.call-done = (f32[384,128]{1,0:T(8,128)}, f32[128,128]{1,0:T(8,128)}, f32[256,128]{1,0:T(8,128)}, f32[128,128]{1,0:T(8,128)}) async-done(((f32[384,128]{1,0:T(8,128)}, f32[128,128]{1,0:T(8,128)}, f32[256,128]{1,0:T(8,128)}, f32[128,128]{1,0:T(8,128)}), (f32[384,128]{1,0:T(8,128)}, f32[128,128]{1,0:T(8,128)}, f32[256,128]{1,0:T(8,128)}, ...) | async-done | bytes 458768 | tf_op jit(solution)/shard_map/psum | solution.py:206
  1020.5 2.1 fusion.146
  1022.6 41.9 %all-reduce.7.cloned.1.call-done = (f32[384,128]{1,0:T(8,128)}, f32[128,128]{1,0:T(8,128)}, f32[256,128]{1,0:T(8,128)}, f32[128,128]{1,0:T(8,128)}) async-done(((f32[384,128]{1,0:T(8,128)}, f32[128,128]{1,0:T(8,128)}, f32[256,128]{1,0:T(8,128)}, f32[128,128]{1,0:T(8,128)}), (f32[384,128]{1,0:T(8,128)}, f32[128,128]{1,0:T(8,128)}, f32[256,128]{1,0:T(8,128)}, ...) | async-done | bytes 458768 | tf_op jit(solution)/shard_map/psum | solution.py:206
  1064.5 1.7 broadcast_multiply_fusion.8
  (1109 shorter events, 244.1 us)
Async XLA Ops:
  7.2 131.1 %copy-start = (bf16[256,128]{1,0:T(8,128)(2,1)S(1)}, bf16[256,128]{1,0:T(8,128)(2,1)}, u32[]{:S(2)}) copy-start(bf16[256,128]{1,0:T(8,128)(2,1)} %param.36) | copy-start | bytes 196612
  7.2 1011.5 %all-reduce.5.cloned.1.call-start = ((), (), s32[]{:S(2)}) async-start(), calls=%async_computation | async-start | bytes 917504 | tf_op jit(solution)/shard_map/psum | solution.py:206
  7.2 42.2 %collective-permute-start = (bf16[1024,128]{1,0:T(8,128)(2,1)}, bf16[1024,128]{1,0:T(8,128)(2,1)}, u32[]{:S(2)}, u32[]{:S(2)}) collective-permute-start(bf16[1024,128]{1,0:T(8,128)(2,1)} %bitcast.285), channel_id=1, source_target_pairs={{0,64},{64,128},{128,192},{1,65},{65,129},{129,193},{2,66},{66,130... | collective-permute-start | bytes 786440 | tf_op jit(solution)/shard_map/ppermute | solution.py:12
  9.7 69.4 %collective-permute-start.1 = (bf16[1024,128]{1,0:T(8,128)(2,1)}, bf16[1024,128]{1,0:T(8,128)(2,1)}, u32[]{:S(2)}, u32[]{:S(2)}) collective-permute-start(bf16[1024,128]{1,0:T(8,128)(2,1)} %bitcast.286), channel_id=1, source_target_pairs={{63,0},{0,1},{1,2},{2,3},{3,4},{4,5},{5,6},{6,7},{7,8},{8,9},{9,10... | collective-permute-start | bytes 786440 | tf_op jit(solution)/shard_map/ppermute | solution.py:18
  11.2 97.6 %collective-permute-start.2 = (bf16[1024,128]{1,0:T(8,128)(2,1)}, bf16[1024,128]{1,0:T(8,128)(2,1)}, u32[]{:S(2)}, u32[]{:S(2)}) collective-permute-start(bf16[1024,128]{1,0:T(8,128)(2,1)} %bitcast.287), channel_id=1, source_target_pairs={{1,0},{2,1},{3,2},{4,3},{5,4},{6,5},{7,6},{8,7},{9,8},{10,9},{11,1... | collective-permute-start | bytes 786440 | tf_op jit(solution)/shard_map/ppermute | solution.py:18
  14.9 1.6 copy-start.25
  16.7 31.7 %copy-start.3 = (bf16[1,1,4,1024,128]{4,3,2,1,0:T(8,128)(2,1)S(1)}, bf16[1,1,4,1024,128]{4,3,2,1,0:T(8,128)(2,1)}, u32[]{:S(2)}) copy-start(bf16[1,1,4,1024,128]{4,3,2,1,0:T(8,128)(2,1)} %param.33) | copy-start | bytes 3145732
  16.7 3.4 copy-start.58
  22.0 1.7 copy-start.18
  22.0 1.7 copy-start.20
  24.7 3.4 copy-start.58
  29.9 1.7 copy-start.18
  29.9 1.7 copy-start.20
  32.6 3.3 copy-start.58
  37.8 1.7 copy-start.18
  37.8 1.7 copy-start.20
  40.5 3.4 copy-start.58
  45.8 1.7 copy-start.18
  45.8 1.7 copy-start.20
  144.5 6.3 copy-start.50
  152.0 1.4 copy-start.49
  157.6 6.3 copy-start.50
  165.1 2.4 copy-start.49
  171.7 6.3 copy-start.50
  179.2 2.4 copy-start.49
  185.8 6.3 copy-start.50
  193.3 2.4 copy-start.49
  200.0 3.3 copy-start.52
  204.5 1.4 copy-start.43
  210.1 3.3 copy-start.52
  214.7 2.4 copy-start.43
  221.3 3.3 copy-start.52
  225.9 2.4 copy-start.43
  232.5 3.3 copy-start.52
  237.1 2.4 copy-start.43
  243.7 3.3 copy-start.54
  248.2 1.4 copy-start.45
  253.8 3.3 copy-start.54
  258.4 2.4 copy-start.45
  265.0 3.3 copy-start.54
  269.6 2.4 copy-start.45
  276.2 3.3 copy-start.54
  280.8 2.4 copy-start.45
  287.4 3.3 copy-start.56
  291.9 1.4 copy-start.47
  297.5 3.3 copy-start.56
  302.1 2.4 copy-start.47
  308.7 3.3 copy-start.56
  313.2 2.4 copy-start.47
  319.8 3.3 copy-start.56
  324.4 2.4 copy-start.47
  330.9 4.0 copy-start.6
  331.6 732.9 %all-reduce.7.cloned.1.call-start = ((), (), s32[]{:S(2)}) async-start(), calls=%async_computation.1 | async-start | bytes 917504 | tf_op jit(solution)/shard_map/psum | solution.py:206
  333.5 9.9 copy-start.7
  333.5 686.4 %collective-permute-start.5 = (bf16[1024,128]{1,0:T(8,128)(2,1)}, bf16[1024,128]{1,0:T(8,128)(2,1)}, u32[]{:S(2)}, u32[]{:S(2)}) collective-permute-start(bf16[1024,128]{1,0:T(8,128)(2,1)} %convert_element_type.565), channel_id=1, source_target_pairs={{63,0},{0,1},{1,2},{2,3},{3,4},{4,5},{5,6},{6,7},{7,8},{8,9},{9,10... | collective-permute-start | bytes 786440 | tf_op jit(solution)/shard_map/ppermute | solution.py:18
  335.7 684.2 %collective-permute-start.4 = (bf16[1024,128]{1,0:T(8,128)(2,1)}, bf16[1024,128]{1,0:T(8,128)(2,1)}, u32[]{:S(2)}, u32[]{:S(2)}) collective-permute-start(bf16[1024,128]{1,0:T(8,128)(2,1)} %convert_element_type.563), channel_id=1, source_target_pairs={{1,0},{2,1},{3,2},{4,3},{5,4},{6,5},{7,6},{8,7},{9,8},{10,9},{11,1... | collective-permute-start | bytes 786440 | tf_op jit(solution)/shard_map/ppermute | solution.py:18
  343.4 675.3 %copy-start.22 = (bf16[1024,128]{1,0:T(8,128)(2,1)S(1)}, bf16[1024,128]{1,0:T(8,128)(2,1)}, u32[]{:S(2)}) copy-start(bf16[1024,128]{1,0:T(8,128)(2,1)} %get-tuple-element.2003) | copy-start | bytes 786436
  343.4 675.3 %copy-start.23 = (bf16[1024,128]{1,0:T(8,128)(2,1)S(1)}, bf16[1024,128]{1,0:T(8,128)(2,1)}, u32[]{:S(2)}) copy-start(bf16[1024,128]{1,0:T(8,128)(2,1)} %get-tuple-element.2002) | copy-start | bytes 786436
  343.4 675.3 %copy-start.24 = (bf16[1024,128]{1,0:T(8,128)(2,1)S(1)}, bf16[1024,128]{1,0:T(8,128)(2,1)}, u32[]{:S(2)}) copy-start(bf16[1024,128]{1,0:T(8,128)(2,1)} %get-tuple-element.2001) | copy-start | bytes 786436
  344.1 674.6 %copy-start.21 = (bf16[1024,128]{1,0:T(8,128)(2,1)S(1)}, bf16[1024,128]{1,0:T(8,128)(2,1)}, u32[]{:S(2)}) copy-start(bf16[1024,128]{1,0:T(8,128)(2,1)} %get-tuple-element.2004) | copy-start | bytes 786436
  344.1 675.7 %collective-permute-start.3 = (bf16[1024,128]{1,0:T(8,128)(2,1)}, bf16[1024,128]{1,0:T(8,128)(2,1)}, u32[]{:S(2)}, u32[]{:S(2)}) collective-permute-start(bf16[1024,128]{1,0:T(8,128)(2,1)} %convert_element_type.561), channel_id=1, source_target_pairs={{64,0},{128,64},{192,128},{65,1},{129,65},{193,129},{66,2},{130,66... | collective-permute-start | bytes 786440 | tf_op jit(solution)/shard_map/ppermute | solution.py:12
  1018.7 1.8 copy-start.14
  1018.7 1.8 copy-start.29
  1064.5 1.7 copy-start.60
  (159 other events, 134.1 us)
Sparse Core Ops, SparseCore 0:
  331.8 686.8 all-reduce.4
  1021.6 42.9 all-reduce.6
